TPU v7x, 256 devices: a whole 4x4x8 slice. The times are simulated.
256 devices in a mesh: occ: 16 (over z_lo, y), aux: 16 (over z_hi, x, core).
Axes of the slice: x: 4, y: 4, z: 8 (z_hi: 2, z_lo: 4; z = z_hi * 4 + z_lo), core: 2. Of those that a mesh axis runs over, the one named last changes fastest.
Arguments:
- factors: bfloat16 [8192, 32, 1024], P('aux', 'occ'), may hold values from -16 to 16
- partner: bfloat16 [8192, 1024], P('aux', 'occ'), may hold values from -0.09375 to 0.09375
- occupied_energy: float32 [32], P('occ'), may hold values from -2 to -0.5
- partner_energy: float32 [1], replicated, may hold values from -3 to -0.3
- virtual_energy: float32 [1024], replicated, may hold values from 0.2 to 3
Outputs:
- amplitudes: bfloat16 [32768, 1024], P(('occ', 'aux'))
- density_factors: bfloat16 [8192, 32, 1024], P('aux', 'occ')
All inputs are finite; a program needn't handle non-finite values.
Results may differ from a plain program's by a relative error of at most 0.015.
Values may be sent and summed in bfloat16 or wider, within the bound.
A program may use at most 64 MiB of HBM per device.

v0:
```python
import jax
import jax.numpy as jnp
from jax import lax
from jax.sharding import PartitionSpec as P


def lookup(entries, indices):
    positions = jnp.arange(entries.shape[0], dtype=jnp.int32)
    matches = indices[:, None] == positions[None, :]
    return jnp.sum(jnp.where(matches, entries[None, :], 0.0), axis=1)


def shards(factors, partner, occupied_energy, partner_energy, virtual_energy):
    aux_rows, local_occ, virt_count = factors.shape
    partner_full = lax.all_gather(partner, "occ", axis=1, tiled=True)
    flat_factors = factors.reshape(aux_rows, local_occ * virt_count)
    total_rows = local_occ * virt_count
    row_share = total_rows // lax.axis_size("aux")
    own_first = lax.axis_index("aux") * row_share
    integrals = lax.psum_scatter(
        lax.dot_general(
            flat_factors, partner_full, (((0,), (0,)), ((), ())), preferred_element_type=jnp.float32
        ).astype(jnp.bfloat16),
        "aux",
        scatter_dimension=0,
        tiled=True,
    ).astype(jnp.float32)
    row_ids = own_first + jnp.arange(row_share, dtype=jnp.int32)
    occ_part = lookup(occupied_energy, row_ids // virt_count)
    virt_part = lookup(virtual_energy, row_ids % virt_count)
    divisor = virt_part[:, None] + virtual_energy[None, :] - occ_part[:, None] - partner_energy[0]
    amp_shard = (-integrals / divisor).astype(jnp.bfloat16)
    amp_full = lax.all_gather(amp_shard, "aux", axis=0, tiled=True)
    amp_cube = amp_full.reshape(local_occ, virt_count, virt_count)
    direct = jnp.einsum("qb,iab->qia", partner_full, amp_cube, preferred_element_type=jnp.float32)
    swapped = jnp.einsum("qb,iba->qia", partner_full, amp_cube, preferred_element_type=jnp.float32)
    density = (2.0 * direct - swapped).astype(jnp.bfloat16)
    return (amp_shard, density)


def solution(mesh):
    return jax.shard_map(
        shards,
        mesh=mesh,
        in_specs=(P("aux", "occ", None), P("aux", "occ"), P("occ"), P(), P()),
        out_specs=(P(("occ", "aux"), None), P("aux", "occ", None)),
        check_vma=False,
    )
```

profile of v0, /device:TPU:1, one launch (start us, length us, event | category | flops | bytes accessed | tf_op | source)
XLA Modules:
  0.0 296.8 jit_solution(7066231302340933514)
XLA Ops:
  7.2 0.0 all-gather.3.cloned.1.call-start
  7.2 0.7 all-gather.3.cloned.1.call-update
  7.9 0.0 reduce-scatter.2.cloned.1.call-start
  7.9 2.2 copy.12
  10.1 73.7 %all-gather.3.cloned.1.call-done = bf16[512,1024]{0,1:T(8,128)(2,1)} async-done(((bf16[512,64]{0,1:T(8,128)(2,1)}), bf16[512,1024]{0,1:T(8,128)(2,1)}) %all-gather.3.cloned.1.call-update) | async-done | bytes 1048592 | tf_op jit(solution)/shard_map/all_gather | solution.py:15
  83.9 5.6 %convolution_convert_fusion = bf16[2048,1024]{1,0:T(8,128)(2,1)} fusion(bf16[512,2048]{1,0:T(8,128)(2,1)S(1)} %bitcast.17, bf16[512,1024]{0,1:T(8,128)(2,1)} %all-gather.3.cloned.1.call-done), kind=kOutput, calls=%fused_computation.1 | convolution fusion | flops 2149580800 | bytes 7340032 | tf_op jit(solution)/shard_map/dot_general | solution.py:21
  89.4 0.0 copy-start.3
  89.4 0.0 copy-start
  89.4 0.0 copy-start.2
  89.4 0.0 reduce-scatter.2.cloned.1.call-update
  89.5 0.0 all-gather.5.cloned.1.call-start
  90.3 0.0 copy-done.3
  90.3 0.1 fusion.4
  90.4 0.0 copy-done
  90.4 0.2 select_reduce_fusion
  90.6 110.0 %reduce-scatter.2.cloned.1.call-done = bf16[128,1024]{1,0:T(8,128)(2,1)} async-done(((bf16[2048,1024]{1,0:T(8,128)(2,1)}), bf16[128,1024]{1,0:T(8,128)(2,1)}) %reduce-scatter.2.cloned.1.call-update) | async-done | bytes 262160 | tf_op jit(solution)/shard_map/reduce_scatter | solution.py:20
  200.5 1.9 divide_convert_fusion
  202.4 0.0 all-gather.5.cloned.1.call-update
  202.4 76.8 %all-gather.5.cloned.1.call-done = bf16[2048,1024]{1,0:T(8,128)(2,1)} async-done(((bf16[128,1024]{1,0:T(8,128)(2,1)}), bf16[2048,1024]{1,0:T(8,128)(2,1)}) %all-gather.5.cloned.1.call-update) | async-done | bytes 4194320 | tf_op jit(solution)/shard_map/all_gather | solution.py:33
  279.2 0.0 copy-done.2
  279.2 4.7 %fusion.1 = f32[2,1024,512]{2,1,0:T(8,128)S(1)} fusion(bf16[2,1024,1024]{2,1,0:T(8,128)(2,1)} %bitcast.18, bf16[512,1024]{0,1:T(8,128)(2,1)S(1)} %copy-done.2), kind=kOutput, calls=%fused_computation.3 | convolution fusion | flops 2147483648 | bytes 9437184 | tf_op jit(solution)/shard_map/qb,iba->qia/dot_general | solution.py:36
  283.9 0.0 copy-done.1
  284.0 2.3 fusion
  286.3 3.9 %copy.10 = bf16[512,2,1024]{2,1,0:T(2,128)(2,1)} copy(bf16[512,2,1024]{0,2,1:T(8,128)(2,1)S(1)} %fusion) | data formatting | bytes 4194304
  (2 shorter events, 0.0 us)
Async XLA Ops:
  7.2 76.7 %all-gather.3.cloned.1.call-start = ((), (), s32[]{:S(2)}) async-start(), calls=%async_computation.1 | async-start | bytes 1114112 | tf_op jit(solution)/shard_map/all_gather | solution.py:15
  7.9 192.6 %reduce-scatter.2.cloned.1.call-start = ((), (), s32[]{:S(2)}) async-start(), calls=%async_computation.2 | async-start | bytes 4456448 | tf_op jit(solution)/shard_map/reduce_scatter | solution.py:20
  89.4 0.8 copy-start.3
  89.4 0.9 copy-start
  89.4 189.8 %copy-start.2 = (bf16[512,1024]{0,1:T(8,128)(2,1)S(1)}, bf16[512,1024]{0,1:T(8,128)(2,1)}, u32[]{:S(2)}) copy-start(bf16[512,1024]{0,1:T(8,128)(2,1)} %all-gather.3.cloned.1.call-done) | copy-start | bytes 3145732
  89.5 189.7 %all-gather.5.cloned.1.call-start = ((), (), s32[]{:S(2)}) async-start(), calls=%async_computation.3 | async-start | bytes 4456448 | tf_op jit(solution)/shard_map/all_gather | solution.py:33
  279.2 4.7 %copy-start.1 = (bf16[2048,1024]{1,0:T(8,128)(2,1)S(1)}, bf16[2048,1024]{1,0:T(8,128)(2,1)}, u32[]{:S(2)}) copy-start(bf16[2048,1024]{1,0:T(8,128)(2,1)} %all-gather.5.cloned.1.call-done) | copy-start | bytes 12582916
Sparse Core Ops, SparseCore 0:
  9.8 74.0 all-gather.2
  89.6 110.8 reduce-scatter.1
  203.8 75.3 all-gather.4
where the time goes:
time: 297 us
  waiting for transfers between devices  261 us (88%)
  between operations  14.5 us (5%)
  matrix products  12.6 us (4%)
  local copies, waits for them, and re-layouts  6.14 us (2%)
    reduce_scatter x1, waiting for transfers between devices, shards(): lax.psum_scatter(lax.dot_general(flat_factors, partner_full, (((0,), (0,)...  110 us
    all_gather x1, waiting for transfers between devices, shards(): amp_full = lax.all_gather(amp_shard, 'aux', axis=0, tiled=True)  76.8 us
    all_gather x1, waiting for transfers between devices, shards(): partner_full = lax.all_gather(partner, 'occ', axis=1, tiled=True)  73.7 us
    unnamed x10, local copies, waits for them, and re-layouts  6.14 us
  transfers between devices with their start and end apart: 3, of which 3 were waited for; matrix products, arithmetic and copies ran while one was open for 1% of the time, Pallas kernels for 0%

commit v1 on v0

--- a/solution.py
+++ b/solution.py
@@ -12,7 +12,10 @@
 
 def shards(factors, partner, occupied_energy, partner_energy, virtual_energy):
     aux_rows, local_occ, virt_count = factors.shape
-    partner_full = lax.all_gather(partner, "occ", axis=1, tiled=True)
+    count = lax.axis_size("occ")
+    parts = jnp.stack([partner for _ in range(count)])
+    parts = lax.all_to_all(parts, "occ", split_axis=0, concat_axis=0)
+    partner_full = jnp.concatenate(parts, axis=1)
     flat_factors = factors.reshape(aux_rows, local_occ * virt_count)
     total_rows = local_occ * virt_count
     row_share = total_rows // lax.axis_size("aux")

time: 297 us -> 249 us (0.84)
  waiting for transfers between devices: 261 us -> 202 us
  starting transfers between devices: 0.12 us -> 9.26 us
    all_gather x1 -> x0, waiting for transfers between devices: 73.7 us -> none  [shards(): partner_full = lax.all_gather(partner, 'occ', axis=1, tiled=True)]
    all_to_all x0 -> x1, waiting for transfers between devices: none -> 20.4 us  [shards(): parts = lax.all_to_all(parts, 'occ', split_axis=0, concat_axis=0)]
    all_to_all x0 -> x1, starting transfers between devices: none -> 9.17 us  [shards(): parts = lax.all_to_all(parts, 'occ', split_axis=0, concat_axis=0)]
    reduce_scatter x1, waiting for transfers between devices: 110 us -> 105 us  [shards(): lax.psum_scatter(lax.dot_general(flat_factors, partner_full, (((0,), (0,)...]
where the time goes in v1:
time: 249 us
  waiting for transfers between devices  202 us (81%)
  between operations  14.8 us (6%)
  matrix products  13 us (5%)
  starting transfers between devices  9.26 us (4%)
  local copies, waits for them, and re-layouts  7.94 us (3%)
    reduce_scatter x1, waiting for transfers between devices, shards(): lax.psum_scatter(lax.dot_general(flat_factors, partner_full, (((0,), (0,)...  105 us
    all_gather x1, waiting for transfers between devices, shards(): amp_full = lax.all_gather(amp_shard, 'aux', axis=0, tiled=True)  76.7 us
    all_to_all x1, waiting for transfers between devices, shards(): parts = lax.all_to_all(parts, 'occ', split_axis=0, concat_axis=0)  20.4 us
    all_to_all x1, starting transfers between devices, shards(): parts = lax.all_to_all(parts, 'occ', split_axis=0, concat_axis=0)  9.17 us
    dot_general x1, matrix products, shards(): lax.dot_general(flat_factors, partner_full, (((0,), (0,)), ((), ())), pre...  5.93 us
    unnamed x10, local copies, waits for them, and re-layouts  5.89 us
  transfers between devices with their start and end apart: 3, of which 3 were waited for; matrix products, arithmetic and copies ran while one was open for 1% of the time, Pallas kernels for 0%

profile of v1, /device:TPU:1, one launch (start us, length us, event | category | flops | bytes accessed | tf_op | source)
XLA Modules:
  0.0 248.8 jit_solution(5234044562125168430)
XLA Ops:
  7.2 0.0 copy-start
  7.2 2.1 stack.2
  9.2 9.2 %all-to-all-start = ((bf16[16,512,64]{1,2,0:T(8,128)(2,1)}), bf16[16,512,64]{1,2,0:T(8,128)(2,1)S(1)}, u32[]{:S(2)}, u32[]{:S(2)}) async-start(bf16[16,512,64]{1,2,0:T(8,128)(2,1)} %stack.2), calls=%async_computation | async-start | bytes 2097152 | tf_op jit(solution)/shard_map/all_to_all | solution.py:17
  18.4 0.0 reduce-scatter.2.cloned.1.call-start
  18.5 0.0 copy-done
  18.5 1.9 copy.23
  20.4 20.4 %all-to-all-done = bf16[16,512,64]{1,2,0:T(8,128)(2,1)S(1)} async-done(((bf16[16,512,64]{1,2,0:T(8,128)(2,1)}), bf16[16,512,64]{1,2,0:T(8,128)(2,1)S(1)}, u32[]{:S(2)}, u32[]{:S(2)}) %all-to-all-start) | async-done | bytes 1048608 | tf_op jit(solution)/shard_map/all_to_all | solution.py:17
  40.8 5.9 %convolution_convert_fusion = bf16[2048,1024]{1,0:T(8,128)(2,1)} fusion(bf16[512,2048]{1,0:T(8,128)(2,1)} %bitcast.20, bf16[512,1024]{0,1:T(8,128)(2,1)S(1)} %bitcast.21), kind=kOutput, calls=%fused_computation.1 | convolution fusion | flops 2149580800 | bytes 7340032 | tf_op jit(solution)/shard_map/dot_general | solution.py:24
  46.7 0.0 copy-start.3
  46.7 0.0 copy-start.1
  46.7 0.0 reduce-scatter.2.cloned.1.call-update
  46.7 0.0 all-gather.2.cloned.1.call-start
  47.4 0.0 copy-done.3
  47.5 0.1 fusion.1
  47.5 0.0 copy-done.1
  47.5 0.2 select_reduce_fusion
  47.7 104.6 %reduce-scatter.2.cloned.1.call-done = bf16[128,1024]{1,0:T(8,128)(2,1)} async-done(((bf16[2048,1024]{1,0:T(8,128)(2,1)}), bf16[128,1024]{1,0:T(8,128)(2,1)}) %reduce-scatter.2.cloned.1.call-update) | async-done | bytes 262160 | tf_op jit(solution)/shard_map/reduce_scatter | solution.py:23
  152.3 1.9 divide_convert_fusion
  154.2 0.0 all-gather.2.cloned.1.call-update
  154.2 76.7 %all-gather.2.cloned.1.call-done = bf16[2048,1024]{1,0:T(8,128)(2,1)} async-done(((bf16[128,1024]{1,0:T(8,128)(2,1)}), bf16[2048,1024]{1,0:T(8,128)(2,1)}) %all-gather.2.cloned.1.call-update) | async-done | bytes 4194320 | tf_op jit(solution)/shard_map/all_gather | solution.py:36
  230.9 4.7 %fusion.2 = f32[2,1024,512]{2,1,0:T(8,128)S(1)} fusion(bf16[2,1024,1024]{2,1,0:T(8,128)(2,1)} %bitcast.24, bf16[512,1024,1]{0,1,2:T(8,128)(2,1)S(1)} %bitcast.22), kind=kOutput, calls=%fused_computation.14 | convolution fusion | flops 2147483648 | bytes 9437184 | tf_op jit(solution)/shard_map/qb,iba->qia/dot_general | solution.py:39
  235.7 0.0 copy-done.2
  235.7 2.3 fusion
  238.0 3.9 %copy.17 = bf16[512,2,1024]{2,1,0:T(2,128)(2,1)} copy(bf16[512,2,1024]{0,2,1:T(8,128)(2,1)S(1)} %fusion) | data formatting | bytes 4194304
  (2 shorter events, 0.0 us)
Async XLA Ops:
  7.2 11.3 %copy-start = (bf16[512,2,1024]{2,1,0:T(2,128)(2,1)S(1)}, bf16[512,2,1024]{2,1,0:T(2,128)(2,1)}, u32[]{:S(2)}) copy-start(bf16[512,2,1024]{2,1,0:T(2,128)(2,1)} %param.5) | copy-start | bytes 6291460
  9.2 31.5 %all-to-all-start = ((bf16[16,512,64]{1,2,0:T(8,128)(2,1)}), bf16[16,512,64]{1,2,0:T(8,128)(2,1)S(1)}, u32[]{:S(2)}, u32[]{:S(2)}) async-start(bf16[16,512,64]{1,2,0:T(8,128)(2,1)} %stack.2), calls=%async_computation | async-start | bytes 2097152 | tf_op jit(solution)/shard_map/all_to_all | solution.py:17
  18.4 133.9 %reduce-scatter.2.cloned.1.call-start = ((), (), s32[]{:S(2)}) async-start(), calls=%async_computation.2 | async-start | bytes 4456448 | tf_op jit(solution)/shard_map/reduce_scatter | solution.py:23
  46.7 0.8 copy-start.3
  46.7 0.8 copy-start.1
  46.7 184.2 %all-gather.2.cloned.1.call-start = ((), (), s32[]{:S(2)}) async-start(), calls=%async_computation.3 | async-start | bytes 4456448 | tf_op jit(solution)/shard_map/all_gather | solution.py:36
  230.9 4.7 %copy-start.2 = (bf16[2048,1024]{1,0:T(8,128)(2,1)S(1)}, bf16[2048,1024]{1,0:T(8,128)(2,1)}, u32[]{:S(2)}) copy-start(bf16[2048,1024]{1,0:T(8,128)(2,1)} %all-gather.2.cloned.1.call-done) | copy-start | bytes 12582916
Sparse Core Ops, SparseCore 0:
  46.8 105.4 reduce-scatter.1
  155.6 75.2 all-gather.1
